TPU v7x, 32 devices: a whole 2x2x4 slice. The times are simulated.
32 devices in a mesh: dp: 8 (over y, x, core), mp: 4 (over z).
Axes of the slice: x: 2, y: 2, z: 4, core: 2. Of those that a mesh axis runs over, the one named last changes fastest.
Arguments:
- tokens: bfloat16 [8192, 2048], P(('dp', 'mp')), may hold values from -6 to 6
- valid: int32 [8], P('dp'), may hold values from 256 to 1024, as said below
- attn_gain: float32 [2048], replicated, may hold values from 0.25 to 1.75
- w_query: bfloat16 [2048, 2048], replicated, may hold values from -0.125 to 0.125
- w_key: bfloat16 [2048, 2048], replicated, may hold values from -0.125 to 0.125
- w_value: bfloat16 [2048, 2048], replicated, may hold values from -0.125 to 0.125
- w_rank: bfloat16 [2048, 16], replicated, may hold values from -0.125 to 0.125
- w_forget: bfloat16 [16, 256], replicated, may hold values from -1.5 to 1.5
- forget_bias: float32 [256], replicated, may hold values from -2 to 6
- head_gain: float32 [512], replicated, may hold values from 0.25 to 1.75
- w_out: bfloat16 [2048, 2048], replicated, may hold values from -0.125 to 0.125
- mlp_gain: float32 [2048], replicated, may hold values from 0.25 to 1.75
- w_gate: bfloat16 [2048, 5632], P(None, 'mp'), may hold values from -0.125 to 0.125
- w_up: bfloat16 [2048, 5632], P(None, 'mp'), may hold values from -0.125 to 0.125
- w_down: bfloat16 [5632, 2048], P('mp'), may hold values from -0.15625 to 0.15625
- cotangent: bfloat16 [8192, 2048], P(('dp', 'mp')), may hold values from -6 to 6
Outputs:
- output: bfloat16 [8192, 2048], P(('dp', 'mp'))
- grad_tokens: float32 [8192, 2048], P(('dp', 'mp'))
- grad_attn_gain: float32 [2048], P('dp')
- grad_query: float32 [2048, 2048], P('dp', 'mp')
- grad_key: float32 [2048, 2048], P('dp', 'mp')
- grad_value: float32 [2048, 2048], P('dp', 'mp')
- grad_rank: float32 [2048, 16], P('dp')
- grad_forget: float32 [16, 256], P(None, 'dp')
- grad_forget_bias: float32 [256], P('dp')
- grad_head_gain: float32 [512], P('dp')
- grad_out: float32 [2048, 2048], P('dp', 'mp')
- grad_mlp_gain: float32 [2048], P('dp')
- grad_gate: float32 [2048, 5632], P('dp', 'mp')
- grad_up: float32 [2048, 5632], P('dp', 'mp')
- grad_down: float32 [5632, 2048], P('mp', 'dp')
Inputs may be any that keep to these rules, and one draw needn't show every extreme that they name: Each bucket holds one sequence whose first valid tokens count; one bucket is full in every draw.
All inputs are finite; a program needn't handle non-finite values.
Results may differ from a plain program's by a relative error of at most 0.018.
Values may be sent and summed in bfloat16 or wider, within the bound.
No kernel may reach another device: no remote copies, remote signals or barrier semaphores. Data moves between devices by JAX's collectives and lax.ppermute only.
A program may use at most 448 MiB of HBM per device.

v0:
```python
import math
import jax
import jax.numpy as jnp
from jax import lax
from jax.sharding import PartitionSpec as P

HEADS = 4
BLOCK = 128
EPS = 1e-06
GATE_NORM = 8.0
HIGH_PRECISION = lax.Precision.HIGHEST
CONTRACT_ROWS = (((0,), (0,)), ((), ()))
CONTRACT_COLS = (((1,), (1,)), ((), ()))


def rms_norm(values, gain):
    return values * lax.rsqrt(jnp.mean(values * values, axis=-1, keepdims=True) + EPS) * gain


def silu_slope(raw):
    sigmoid = jax.nn.sigmoid(raw)
    return sigmoid * (1.0 + raw * (1.0 - sigmoid))


def rows_product(left, right):
    return lax.dot_general(left, right, CONTRACT_ROWS, preferred_element_type=jnp.float32)


def cols_product(left, right):
    return lax.dot_general(left, right, CONTRACT_COLS, preferred_element_type=jnp.float32)


def piece_step(states, block):
    key_slot_state, value_slot_state = states
    query_rows, key_row_block, value_row_block, log_decay = block
    length = query_rows.shape[0]
    scale = 1.0 / math.sqrt(query_rows.shape[2])
    running_total = jnp.cumsum(log_decay, axis=0)
    fresh = 1.0 - jnp.exp(log_decay)
    causal = (jnp.arange(length)[:, None] >= jnp.arange(length)[None, :])[:, :, None, None]
    spread = running_total[:, None] - running_total[None, :]
    weights = jnp.where(causal, jnp.exp(jnp.where(causal, spread, 0.0)), 0.0) * fresh[None]
    direct = jnp.einsum("thd,jhd->htj", query_rows, key_row_block, precision=HIGH_PRECISION)
    attention_scores = jnp.exp(running_total) * jnp.einsum(
        "cso,sio->csi", query_rows, key_slot_state, precision=HIGH_PRECISION
    )
    attention_scores = (
        attention_scores + jnp.einsum("htj,tjhm->thm", direct, weights, precision=HIGH_PRECISION)
    ) * scale
    attention_probabilities = jax.nn.softmax(attention_scores, axis=-1)
    mixing = jnp.einsum("thm,tjhm->htj", attention_probabilities, weights, precision=HIGH_PRECISION)
    output_rows = jnp.einsum(
        "lwe,wez->lwz",
        attention_probabilities * jnp.exp(running_total),
        value_slot_state,
        precision=HIGH_PRECISION,
    )
    output_rows = output_rows + jnp.einsum(
        "htj,jhd->thd", mixing, value_row_block, precision=HIGH_PRECISION
    )
    final = running_total[-1]
    carried_state = jnp.exp(final[None] - running_total) * fresh
    key_slot_state = jnp.exp(final)[:, :, None] * key_slot_state + jnp.einsum(
        "eoq,eon->oqn", carried_state, key_row_block, precision=HIGH_PRECISION
    )
    value_slot_state = jnp.exp(final)[:, :, None] * value_slot_state + jnp.einsum(
        "eoq,eon->oqn", carried_state, value_row_block, precision=HIGH_PRECISION
    )
    return ((key_slot_state, value_slot_state), output_rows)


def slot_block(states, block):
    length = block[0].shape[0]
    piece_length = min(16, length)
    count = length // piece_length
    pieces = tuple((member.reshape((count, piece_length) + member.shape[1:]) for member in block))
    states, output_rows = lax.scan(piece_step, states, pieces)
    return (states, output_rows.reshape(block[0].shape))


def slot_mixer(query_rows, key_row_block, value_row_block, log_decay):
    steps = query_rows.shape[0] // BLOCK
    blocks = tuple(
        (
            member.reshape((steps, BLOCK) + member.shape[1:])
            for member in (query_rows, key_row_block, value_row_block, log_decay)
        )
    )
    blank_state = jnp.zeros(
        (query_rows.shape[1], log_decay.shape[2], query_rows.shape[2]), jnp.float32
    )
    _, output_rows = lax.scan(jax.checkpoint(slot_block), (blank_state, blank_state), blocks)
    return output_rows.reshape(query_rows.shape)


def local(
    tokens,
    valid,
    attn_gain,
    w_query,
    w_key,
    w_value,
    w_rank,
    w_forget,
    forget_bias,
    head_gain,
    w_out,
    mlp_gain,
    w_gate,
    w_up,
    w_down,
    cotangent,
):
    shard_rows = tokens.shape[0]
    gathered, upstream = (
        lax.all_gather(tokens, "mp", axis=0, tiled=True),
        lax.all_gather(cotangent, "mp", axis=0, tiled=True),
    )
    group_len = gathered.shape[0]
    model_width = w_query.shape[0]
    head_size = model_width // HEADS
    slot_count = forget_bias.shape[0] // HEADS
    shard_index = lax.axis_index("mp")
    column_width = model_width // lax.axis_size("mp")
    own_begin = shard_index * shard_rows
    valid_mask = (jnp.arange(group_len) < valid[0]).astype(jnp.float32)[:, None]
    resid = gathered.astype(jnp.float32)
    normed, pull_first = jax.vjp(rms_norm, resid, attn_gain)
    normed_low = normed.astype(jnp.bfloat16)
    query_raw = jnp.dot(normed_low, w_query, preferred_element_type=jnp.float32)
    key_raw = jnp.dot(normed_low, w_key, preferred_element_type=jnp.float32)
    value_raw = jnp.dot(normed_low, w_value, preferred_element_type=jnp.float32)
    rank_rows = jnp.dot(normed_low, w_rank, preferred_element_type=jnp.float32)
    forget_dense = w_forget.astype(jnp.float32)
    logits = jnp.dot(rank_rows, forget_dense, precision=HIGH_PRECISION) + forget_bias
    log_decay = jax.nn.log_sigmoid(logits) / GATE_NORM

    def heads_view(values, inner_width):
        return values.astype(jnp.float32).reshape(group_len, HEADS, inner_width)

    mixed, pull_slots = jax.vjp(
        slot_mixer,
        heads_view(jax.nn.silu(query_raw).astype(jnp.bfloat16), head_size),
        heads_view(jax.nn.silu(key_raw).astype(jnp.bfloat16), head_size),
        heads_view(value_raw.astype(jnp.bfloat16), head_size),
        heads_view(log_decay, slot_count),
    )
    head_normed, pull_head = jax.vjp(rms_norm, mixed, head_gain)
    head_low = head_normed.reshape(group_len, model_width).astype(jnp.bfloat16)
    hidden_res = resid + jnp.dot(head_low, w_out, preferred_element_type=jnp.float32)
    normed_mlp, pull_second = jax.vjp(rms_norm, hidden_res, mlp_gain)
    mlp_low = normed_mlp.astype(jnp.bfloat16)
    gate_pre = jnp.dot(mlp_low, w_gate, preferred_element_type=jnp.float32)
    up_pre = jnp.dot(mlp_low, w_up, preferred_element_type=jnp.float32)
    activated = jax.nn.silu(gate_pre)
    inner_low = (activated * up_pre).astype(jnp.bfloat16)
    mlp_own = lax.psum_scatter(
        jnp.dot(inner_low, w_down, preferred_element_type=jnp.float32).astype(jnp.bfloat16),
        "mp",
        scatter_dimension=0,
        tiled=True,
    ).astype(jnp.float32)
    own_mask = lax.dynamic_slice_in_dim(valid_mask, own_begin, shard_rows, 0)
    own_hidden = lax.dynamic_slice_in_dim(hidden_res, own_begin, shard_rows, 0)
    output = ((own_hidden + mlp_own) * own_mask).astype(jnp.bfloat16)
    grad_output = upstream.astype(jnp.float32) * valid_mask
    grad_out_low = grad_output.astype(jnp.bfloat16)
    grad_down = rows_product(inner_low, grad_out_low)
    grad_inner = cols_product(grad_out_low, w_down)
    grad_gate_low = (grad_inner * up_pre * silu_slope(gate_pre)).astype(jnp.bfloat16)
    grad_up_low = (grad_inner * activated).astype(jnp.bfloat16)
    grad_gate = rows_product(mlp_low, grad_gate_low)
    grad_up = rows_product(mlp_low, grad_up_low)
    partial_grad = cols_product(grad_gate_low, w_gate) + cols_product(grad_up_low, w_up)
    grad_normed_mlp = lax.psum(partial_grad, "mp")
    grad_res_mlp, grad_mlp_gain = pull_second(grad_normed_mlp)
    grad_hidden = grad_output + grad_res_mlp

    def own_columns(values):
        return lax.dynamic_slice_in_dim(values, shard_index * column_width, column_width, 1)

    grad_hidden_low = grad_hidden.astype(jnp.bfloat16)
    grad_wout = rows_product(head_low, own_columns(grad_hidden_low))
    grad_head_flat = cols_product(grad_hidden_low, w_out)
    grad_mixed, grad_head_gain = pull_head(grad_head_flat.reshape(group_len, HEADS, head_size))
    grad_query_in, grad_key_in, grad_value_in, grad_log_in = pull_slots(grad_mixed)
    grad_query_low = (grad_query_in.reshape(group_len, model_width) * silu_slope(query_raw)).astype(
        jnp.bfloat16
    )
    grad_key_low = (grad_key_in.reshape(group_len, model_width) * silu_slope(key_raw)).astype(
        jnp.bfloat16
    )
    grad_value_low = grad_value_in.reshape(group_len, model_width).astype(jnp.bfloat16)
    grad_logits = (
        grad_log_in.reshape(group_len, HEADS * slot_count) * jax.nn.sigmoid(-logits) / GATE_NORM
    )
    grad_bias = jnp.sum(grad_logits, axis=0)
    grad_forget = lax.dot_general(
        rank_rows,
        grad_logits,
        CONTRACT_ROWS,
        precision=HIGH_PRECISION,
        preferred_element_type=jnp.float32,
    )
    grad_rank_low = lax.dot_general(
        grad_logits,
        forget_dense,
        CONTRACT_COLS,
        precision=HIGH_PRECISION,
        preferred_element_type=jnp.float32,
    ).astype(jnp.bfloat16)
    grad_wrank = rows_product(normed_low, grad_rank_low)
    grad_wquery = rows_product(normed_low, own_columns(grad_query_low))
    grad_wkey = rows_product(normed_low, own_columns(grad_key_low))
    grad_wvalue = rows_product(normed_low, own_columns(grad_value_low))
    grad_normed = cols_product(grad_query_low, w_query) + cols_product(grad_key_low, w_key)
    grad_normed = (
        grad_normed + cols_product(grad_value_low, w_value) + cols_product(grad_rank_low, w_rank)
    )
    grad_resid, grad_attn_gain = pull_first(grad_normed)
    grad_tokens = lax.dynamic_slice_in_dim(grad_hidden + grad_resid, own_begin, shard_rows, 0)
    (
        sum_query,
        sum_key,
        sum_value,
        sum_rank,
        sum_forget,
        sum_bias,
        sum_head_gain,
        sum_wout,
        sum_attn_gain,
        sum_gate,
        sum_up,
        sum_down,
        sum_mlp_gain,
    ) = (
        lax.psum_scatter(grad_wquery, "dp", scatter_dimension=0, tiled=True),
        lax.psum_scatter(grad_wkey, "dp", scatter_dimension=0, tiled=True),
        lax.psum_scatter(grad_wvalue, "dp", scatter_dimension=0, tiled=True),
        lax.psum_scatter(grad_wrank, "dp", scatter_dimension=0, tiled=True),
        lax.psum_scatter(grad_forget, "dp", scatter_dimension=1, tiled=True),
        lax.psum_scatter(grad_bias, "dp", scatter_dimension=0, tiled=True),
        lax.psum_scatter(grad_head_gain, "dp", scatter_dimension=0, tiled=True),
        lax.psum_scatter(grad_wout, "dp", scatter_dimension=0, tiled=True),
        lax.psum_scatter(grad_attn_gain, "dp", scatter_dimension=0, tiled=True),
        lax.psum_scatter(grad_gate, "dp", scatter_dimension=0, tiled=True),
        lax.psum_scatter(grad_up, "dp", scatter_dimension=0, tiled=True),
        lax.psum_scatter(grad_down, "dp", scatter_dimension=1, tiled=True),
        lax.psum_scatter(grad_mlp_gain, "dp", scatter_dimension=0, tiled=True),
    )
    return (
        output,
        grad_tokens,
        sum_attn_gain,
        sum_query,
        sum_key,
        sum_value,
        sum_rank,
        sum_forget,
        sum_bias,
        sum_head_gain,
        sum_wout,
        sum_mlp_gain,
        sum_gate,
        sum_up,
        sum_down,
    )


def solution(mesh):
    return jax.shard_map(
        local,
        mesh=mesh,
        in_specs=(
            P(("dp", "mp"), None),
            P("dp"),
            P(),
            P(),
            P(),
            P(),
            P(),
            P(),
            P(),
            P(),
            P(),
            P(),
            P(None, "mp"),
            P(None, "mp"),
            P("mp", None),
            P(("dp", "mp"), None),
        ),
        out_specs=(
            P(("dp", "mp"), None),
            P(("dp", "mp"), None),
            P("dp"),
            P("dp", "mp"),
            P("dp", "mp"),
            P("dp", "mp"),
            P("dp", None),
            P(None, "dp"),
            P("dp"),
            P("dp"),
            P("dp", "mp"),
            P("dp"),
            P("dp", "mp"),
            P("dp", "mp"),
            P("mp", "dp"),
        ),
        check_vma=False,
    )
```

profile of v0, /device:TPU:0, one launch (start us, length us, event | category | flops | bytes accessed | tf_op | source)
XLA Modules:
  0.0 5010.8 jit_solution(17685367575077738761)
XLA Ops:
  11.3 81.7 %all-gather.3.cloned.1.call-done = bf16[1024,2048]{1,0:T(8,128)(2,1)} async-done(((bf16[256,2048]{1,0:T(8,128)(2,1)}), bf16[1024,2048]{1,0:T(8,128)(2,1)}) %all-gather.3.cloned.1.call-update) | async-done | bytes 4194320 | tf_op jit(solution)/shard_map/all_gather | solution.py:116
  104.5 17.5 fusion.173
  122.0 10.9 reshape.458
  132.9 9.3 copy.325
  142.2 15.3 fusion.174
  157.5 11.1 reshape.459
  168.6 9.3 copy.326
  177.9 13.3 convert_convert_fusion
  191.2 10.9 reshape.460
  202.0 9.2 copy.327
  217.7 780.5 %while.238 = (s32[]{:T(128)}, f32[4,64,512]{2,1,0:T(8,128)}, f32[4,64,512]{2,1,0:T(8,128)}, f32[8,128,4,512]{3,2,1,0:T(4,128)}, f32[8,4,64,512]{3,2,1,0:T(8,128)...) while((s32[]{:T(128)}, f32[4,64,512]{2,1,0:T(8,128)}, ...), condition=%wide.region_7.8_spmd.clone.clone, body=%wide.region_1.7_spmd.clone.clone.sunk | while | flops 115744832 | bytes 20931168 | solution.py:92
  226.3 83.2 %while.241 = (s32[]{:T(128)}, f32[4,64,512]{2,1,0:T(8,128)S(1)}, f32[4,64,512]{2,1,0:T(8,128)S(1)}, f32[8,16,4,512]{3,2,1,0:T(4,128)}, f32[8,16,4,64]{3,2,1,0:T(...) while((s32[]{:T(128)}, f32[4,64,512]{2,1,0:T(8,128)S(1)}, ...), condition=%wide.region_6.6_spmd.clone, body=%wide.region_2.5_spmd.clone.sunk | while | flops 115744832 | bytes 5921913 | solution.py:77
  323.8 83.2 %while.241 = (s32[]{:T(128)}, f32[4,64,512]{2,1,0:T(8,128)S(1)}, f32[4,64,512]{2,1,0:T(8,128)S(1)}, f32[8,16,4,512]{3,2,1,0:T(4,128)}, f32[8,16,4,64]{3,2,1,0:T(...) while((s32[]{:T(128)}, f32[4,64,512]{2,1,0:T(8,128)S(1)}, ...), condition=%wide.region_6.6_spmd.clone, body=%wide.region_2.5_spmd.clone.sunk | while | flops 115744832 | bytes 5921913 | solution.py:77
  421.2 83.2 %while.241 = (s32[]{:T(128)}, f32[4,64,512]{2,1,0:T(8,128)S(1)}, f32[4,64,512]{2,1,0:T(8,128)S(1)}, f32[8,16,4,512]{3,2,1,0:T(4,128)}, f32[8,16,4,64]{3,2,1,0:T(...) while((s32[]{:T(128)}, f32[4,64,512]{2,1,0:T(8,128)S(1)}, ...), condition=%wide.region_6.6_spmd.clone, body=%wide.region_2.5_spmd.clone.sunk | while | flops 115744832 | bytes 5921913 | solution.py:77
  518.7 83.2 %while.241 = (s32[]{:T(128)}, f32[4,64,512]{2,1,0:T(8,128)S(1)}, f32[4,64,512]{2,1,0:T(8,128)S(1)}, f32[8,16,4,512]{3,2,1,0:T(4,128)}, f32[8,16,4,64]{3,2,1,0:T(...) while((s32[]{:T(128)}, f32[4,64,512]{2,1,0:T(8,128)S(1)}, ...), condition=%wide.region_6.6_spmd.clone, body=%wide.region_2.5_spmd.clone.sunk | while | flops 115744832 | bytes 5921913 | solution.py:77
  616.2 83.2 %while.241 = (s32[]{:T(128)}, f32[4,64,512]{2,1,0:T(8,128)S(1)}, f32[4,64,512]{2,1,0:T(8,128)S(1)}, f32[8,16,4,512]{3,2,1,0:T(4,128)}, f32[8,16,4,64]{3,2,1,0:T(...) while((s32[]{:T(128)}, f32[4,64,512]{2,1,0:T(8,128)S(1)}, ...), condition=%wide.region_6.6_spmd.clone, body=%wide.region_2.5_spmd.clone.sunk | while | flops 115744832 | bytes 5921913 | solution.py:77
  713.7 83.2 %while.241 = (s32[]{:T(128)}, f32[4,64,512]{2,1,0:T(8,128)S(1)}, f32[4,64,512]{2,1,0:T(8,128)S(1)}, f32[8,16,4,512]{3,2,1,0:T(4,128)}, f32[8,16,4,64]{3,2,1,0:T(...) while((s32[]{:T(128)}, f32[4,64,512]{2,1,0:T(8,128)S(1)}, ...), condition=%wide.region_6.6_spmd.clone, body=%wide.region_2.5_spmd.clone.sunk | while | flops 115744832 | bytes 5921913 | solution.py:77
  811.2 83.2 %while.241 = (s32[]{:T(128)}, f32[4,64,512]{2,1,0:T(8,128)S(1)}, f32[4,64,512]{2,1,0:T(8,128)S(1)}, f32[8,16,4,512]{3,2,1,0:T(4,128)}, f32[8,16,4,64]{3,2,1,0:T(...) while((s32[]{:T(128)}, f32[4,64,512]{2,1,0:T(8,128)S(1)}, ...), condition=%wide.region_6.6_spmd.clone, body=%wide.region_2.5_spmd.clone.sunk | while | flops 115744832 | bytes 5921913 | solution.py:77
  908.8 83.2 %while.241 = (s32[]{:T(128)}, f32[4,64,512]{2,1,0:T(8,128)S(1)}, f32[4,64,512]{2,1,0:T(8,128)S(1)}, f32[8,16,4,512]{3,2,1,0:T(4,128)}, f32[8,16,4,64]{3,2,1,0:T(...) while((s32[]{:T(128)}, f32[4,64,512]{2,1,0:T(8,128)S(1)}, ...), condition=%wide.region_6.6_spmd.clone, body=%wide.region_2.5_spmd.clone.sunk | while | flops 115744832 | bytes 5921913 | solution.py:77
  1020.1 11.9 mul.733
  1032.0 14.3 multiply_reduce_fusion.6
  1052.0 8.4 fusion.208
  1060.4 10.3 fusion.209
  1070.7 16.2 multiply_convert_fusion.7
  1086.9 10.8 fusion.210
  1097.7 10.7 convolution_add_fusion.9
  1111.7 11.6 convolution_convert_fusion
  1123.4 274.7 %all-reduce.8.cloned.1.call-done = f32[1024,2048]{1,0:T(8,128)} async-done(((f32[1024,2048]{1,0:T(8,128)}), f32[1024,2048]{1,0:T(8,128)}) %all-reduce.8.cloned.1.call-update) | async-done | bytes 8388624 | tf_op jit(solution)/shard_map/psum | solution.py:175
  1408.3 8.8 fusion.204
  1417.2 15.2 multiply_reduce_fusion.1
  1432.3 10.9 reshape.446
  1443.2 8.3 multiply_reduce_fusion.4
  1452.0 10.3 add_add_fusion
  1473.6 2958.0 %while.236 = (s32[]{:T(128)}, f32[4,64,512]{2,1,0:T(8,128)S(1)}, f32[4,64,512]{2,1,0:T(8,128)S(1)}, f32[8,128,4,512]{3,2,1,0:T(4,128)}, f32[8,128,4,512]{3,2,1,0...) while((s32[]{:T(128)}, f32[4,64,512]{2,1,0:T(8,128)S(1)}, ...), condition=%wide.region_30.31_spmd, body=%wide.region_14.0_spmd.sunk | while | flops 314950080 | bytes 50768096 | solution.py:92
  1489.9 117.2 %while.239 = (s32[]{:T(128)}, f32[4,64,512]{2,1,0:T(8,128)S(1)}, f32[4,64,512]{2,1,0:T(8,128)S(1)}, f32[8,4,64]{2,1,0:T(4,128)S(1)}, f32[8,4,64,512]{3,2,1,0:T(8...) while((s32[]{:T(128)}, f32[4,64,512]{2,1,0:T(8,128)S(1)}, ...), condition=%wide.region_19.19_spmd.clone.clone, body=%wide.region_15.18_spmd.clone.clone.sunk | while | flops 84529344 | bytes 8700445 | solution.py:77
  1610.3 227.5 %while.240 = (s32[]{:T(128)}, f32[4,64,512]{2,1,0:T(8,128)S(1)}, f32[4,64,512]{2,1,0:T(8,128)S(1)}, f32[8,16,4,512]{3,2,1,0:T(4,128)}, f32[8,16,4,512]{3,2,1,0:T...) while((s32[]{:T(128)}, f32[4,64,512]{2,1,0:T(8,128)S(1)}, ...), condition=%wide.region_29.29_spmd.clone.clone, body=%wide.region_20.28_spmd.clone.clone.sunk | while | flops 230158336 | bytes 13886109 | solution.py:77
  1859.6 117.2 %while.239 = (s32[]{:T(128)}, f32[4,64,512]{2,1,0:T(8,128)S(1)}, f32[4,64,512]{2,1,0:T(8,128)S(1)}, f32[8,4,64]{2,1,0:T(4,128)S(1)}, f32[8,4,64,512]{3,2,1,0:T(8...) while((s32[]{:T(128)}, f32[4,64,512]{2,1,0:T(8,128)S(1)}, ...), condition=%wide.region_19.19_spmd.clone.clone, body=%wide.region_15.18_spmd.clone.clone.sunk | while | flops 84529344 | bytes 8700445 | solution.py:77
  1980.0 227.5 %while.240 = (s32[]{:T(128)}, f32[4,64,512]{2,1,0:T(8,128)S(1)}, f32[4,64,512]{2,1,0:T(8,128)S(1)}, f32[8,16,4,512]{3,2,1,0:T(4,128)}, f32[8,16,4,512]{3,2,1,0:T...) while((s32[]{:T(128)}, f32[4,64,512]{2,1,0:T(8,128)S(1)}, ...), condition=%wide.region_29.29_spmd.clone.clone, body=%wide.region_20.28_spmd.clone.clone.sunk | while | flops 230158336 | bytes 13886109 | solution.py:77
  2229.3 117.2 %while.239 = (s32[]{:T(128)}, f32[4,64,512]{2,1,0:T(8,128)S(1)}, f32[4,64,512]{2,1,0:T(8,128)S(1)}, f32[8,4,64]{2,1,0:T(4,128)S(1)}, f32[8,4,64,512]{3,2,1,0:T(8...) while((s32[]{:T(128)}, f32[4,64,512]{2,1,0:T(8,128)S(1)}, ...), condition=%wide.region_19.19_spmd.clone.clone, body=%wide.region_15.18_spmd.clone.clone.sunk | while | flops 84529344 | bytes 8700445 | solution.py:77
  2349.8 227.5 %while.240 = (s32[]{:T(128)}, f32[4,64,512]{2,1,0:T(8,128)S(1)}, f32[4,64,512]{2,1,0:T(8,128)S(1)}, f32[8,16,4,512]{3,2,1,0:T(4,128)}, f32[8,16,4,512]{3,2,1,0:T...) while((s32[]{:T(128)}, f32[4,64,512]{2,1,0:T(8,128)S(1)}, ...), condition=%wide.region_29.29_spmd.clone.clone, body=%wide.region_20.28_spmd.clone.clone.sunk | while | flops 230158336 | bytes 13886109 | solution.py:77
  2599.0 117.2 %while.239 = (s32[]{:T(128)}, f32[4,64,512]{2,1,0:T(8,128)S(1)}, f32[4,64,512]{2,1,0:T(8,128)S(1)}, f32[8,4,64]{2,1,0:T(4,128)S(1)}, f32[8,4,64,512]{3,2,1,0:T(8...) while((s32[]{:T(128)}, f32[4,64,512]{2,1,0:T(8,128)S(1)}, ...), condition=%wide.region_19.19_spmd.clone.clone, body=%wide.region_15.18_spmd.clone.clone.sunk | while | flops 84529344 | bytes 8700445 | solution.py:77
  2719.4 227.5 %while.240 = (s32[]{:T(128)}, f32[4,64,512]{2,1,0:T(8,128)S(1)}, f32[4,64,512]{2,1,0:T(8,128)S(1)}, f32[8,16,4,512]{3,2,1,0:T(4,128)}, f32[8,16,4,512]{3,2,1,0:T...) while((s32[]{:T(128)}, f32[4,64,512]{2,1,0:T(8,128)S(1)}, ...), condition=%wide.region_29.29_spmd.clone.clone, body=%wide.region_20.28_spmd.clone.clone.sunk | while | flops 230158336 | bytes 13886109 | solution.py:77
  2968.7 117.2 %while.239 = (s32[]{:T(128)}, f32[4,64,512]{2,1,0:T(8,128)S(1)}, f32[4,64,512]{2,1,0:T(8,128)S(1)}, f32[8,4,64]{2,1,0:T(4,128)S(1)}, f32[8,4,64,512]{3,2,1,0:T(8...) while((s32[]{:T(128)}, f32[4,64,512]{2,1,0:T(8,128)S(1)}, ...), condition=%wide.region_19.19_spmd.clone.clone, body=%wide.region_15.18_spmd.clone.clone.sunk | while | flops 84529344 | bytes 8700445 | solution.py:77
  3089.1 227.5 %while.240 = (s32[]{:T(128)}, f32[4,64,512]{2,1,0:T(8,128)S(1)}, f32[4,64,512]{2,1,0:T(8,128)S(1)}, f32[8,16,4,512]{3,2,1,0:T(4,128)}, f32[8,16,4,512]{3,2,1,0:T...) while((s32[]{:T(128)}, f32[4,64,512]{2,1,0:T(8,128)S(1)}, ...), condition=%wide.region_29.29_spmd.clone.clone, body=%wide.region_20.28_spmd.clone.clone.sunk | while | flops 230158336 | bytes 13886109 | solution.py:77
  3338.3 117.2 %while.239 = (s32[]{:T(128)}, f32[4,64,512]{2,1,0:T(8,128)S(1)}, f32[4,64,512]{2,1,0:T(8,128)S(1)}, f32[8,4,64]{2,1,0:T(4,128)S(1)}, f32[8,4,64,512]{3,2,1,0:T(8...) while((s32[]{:T(128)}, f32[4,64,512]{2,1,0:T(8,128)S(1)}, ...), condition=%wide.region_19.19_spmd.clone.clone, body=%wide.region_15.18_spmd.clone.clone.sunk | while | flops 84529344 | bytes 8700445 | solution.py:77
  3458.7 227.5 %while.240 = (s32[]{:T(128)}, f32[4,64,512]{2,1,0:T(8,128)S(1)}, f32[4,64,512]{2,1,0:T(8,128)S(1)}, f32[8,16,4,512]{3,2,1,0:T(4,128)}, f32[8,16,4,512]{3,2,1,0:T...) while((s32[]{:T(128)}, f32[4,64,512]{2,1,0:T(8,128)S(1)}, ...), condition=%wide.region_29.29_spmd.clone.clone, body=%wide.region_20.28_spmd.clone.clone.sunk | while | flops 230158336 | bytes 13886109 | solution.py:77
  3708.0 117.2 %while.239 = (s32[]{:T(128)}, f32[4,64,512]{2,1,0:T(8,128)S(1)}, f32[4,64,512]{2,1,0:T(8,128)S(1)}, f32[8,4,64]{2,1,0:T(4,128)S(1)}, f32[8,4,64,512]{3,2,1,0:T(8...) while((s32[]{:T(128)}, f32[4,64,512]{2,1,0:T(8,128)S(1)}, ...), condition=%wide.region_19.19_spmd.clone.clone, body=%wide.region_15.18_spmd.clone.clone.sunk | while | flops 84529344 | bytes 8700445 | solution.py:77
  3828.4 227.5 %while.240 = (s32[]{:T(128)}, f32[4,64,512]{2,1,0:T(8,128)S(1)}, f32[4,64,512]{2,1,0:T(8,128)S(1)}, f32[8,16,4,512]{3,2,1,0:T(4,128)}, f32[8,16,4,512]{3,2,1,0:T...) while((s32[]{:T(128)}, f32[4,64,512]{2,1,0:T(8,128)S(1)}, ...), condition=%wide.region_29.29_spmd.clone.clone, body=%wide.region_20.28_spmd.clone.clone.sunk | while | flops 230158336 | bytes 13886109 | solution.py:77
  4077.7 117.2 %while.239 = (s32[]{:T(128)}, f32[4,64,512]{2,1,0:T(8,128)S(1)}, f32[4,64,512]{2,1,0:T(8,128)S(1)}, f32[8,4,64]{2,1,0:T(4,128)S(1)}, f32[8,4,64,512]{3,2,1,0:T(8...) while((s32[]{:T(128)}, f32[4,64,512]{2,1,0:T(8,128)S(1)}, ...), condition=%wide.region_19.19_spmd.clone.clone, body=%wide.region_15.18_spmd.clone.clone.sunk | while | flops 84529344 | bytes 8700445 | solution.py:77
  4198.1 227.5 %while.240 = (s32[]{:T(128)}, f32[4,64,512]{2,1,0:T(8,128)S(1)}, f32[4,64,512]{2,1,0:T(8,128)S(1)}, f32[8,16,4,512]{3,2,1,0:T(4,128)}, f32[8,16,4,512]{3,2,1,0:T...) while((s32[]{:T(128)}, f32[4,64,512]{2,1,0:T(8,128)S(1)}, ...), condition=%wide.region_29.29_spmd.clone.clone, body=%wide.region_20.28_spmd.clone.clone.sunk | while | flops 230158336 | bytes 13886109 | solution.py:77
  4444.3 8.1 fusion.180
  4503.4 11.9 fusion.214
  4515.4 12.1 fusion.215
  4528.2 11.5 fusion.176
  4549.6 12.8 fusion.212
  4562.4 13.4 fusion.211
  4575.8 14.4 fusion.213
  4590.2 10.4 multiply_reduce_fusion.2
  4600.6 24.5 all-reduce.5
  4637.5 38.2 reduce-scatter.15.cloned.1.call-done
  4675.7 55.0 %reduce-scatter.19.cloned.1.call-done = f32[256,512]{1,0:T(8,128)} async-done(((f32[2048,512]{1,0:T(8,128)}), f32[256,512]{1,0:T(8,128)}) %reduce-scatter.19.cloned.1.call-update) | async-done | bytes 524304 | tf_op jit(solution)/shard_map/reduce_scatter | solution.py:239
  4730.7 91.3 %reduce-scatter.25.cloned.1.call-done = f32[256,1408]{1,0:T(8,128)} async-done(((f32[2048,1408]{1,0:T(8,128)}), f32[256,1408]{1,0:T(8,128)}) %reduce-scatter.25.cloned.1.call-update) | async-done | bytes 1441808 | tf_op jit(solution)/shard_map/reduce_scatter | solution.py:246
  4822.0 91.1 %reduce-scatter.27.cloned.1.call-done = f32[256,1408]{1,0:T(8,128)} async-done(((f32[2048,1408]{1,0:T(8,128)}), f32[256,1408]{1,0:T(8,128)}) %reduce-scatter.27.cloned.1.call-update) | async-done | bytes 1441808 | tf_op jit(solution)/shard_map/reduce_scatter | solution.py:247
  4913.0 91.0 %reduce-scatter.29.cloned.1.call-done = f32[1408,256]{1,0:T(8,128)} async-done(((f32[1408,2048]{1,0:T(8,128)}), f32[1408,256]{1,0:T(8,128)}) %reduce-scatter.29.cloned.1.call-update) | async-done | bytes 1441808 | tf_op jit(solution)/shard_map/reduce_scatter | solution.py:248
  (5791 shorter events, 3873.7 us)
Async XLA Ops:
  7.2 89.6 %copy-start = (bf16[2048,16]{0,1:T(8,128)(2,1)S(1)}, bf16[2048,16]{0,1:T(8,128)(2,1)}, u32[]{:S(2)}) copy-start(bf16[2048,16]{0,1:T(8,128)(2,1)} %param.32) | copy-start | bytes 196612
  7.2 85.9 %all-gather.3.cloned.1.call-start = ((), (), s32[]{:S(2)}) async-start(), calls=%async_computation.10 | async-start | bytes 5242880 | tf_op jit(solution)/shard_map/all_gather | solution.py:116
  7.9 92.3 %copy-start.33 = (bf16[16,256]{1,0:T(8,128)(2,1)S(1)}, bf16[16,256]{1,0:T(8,128)(2,1)}, u32[]{:S(2)}) copy-start(bf16[16,256]{1,0:T(8,128)(2,1)} %param.33) | copy-start | bytes 24580
  7.9 92.3 %copy-start.41 = (f32[256]{0:T(256)S(1)}, f32[256]{0:T(256)}, u32[]{:S(2)}) copy-start(f32[256]{0:T(256)} %param.34) | copy-start | bytes 3076
  8.0 1062.7 %all-gather.5.cloned.1.call-start = ((), (), s32[]{:S(2)}) async-start(), calls=%async_computation.12 | async-start | bytes 5242880 | tf_op jit(solution)/shard_map/all_gather | solution.py:117
  8.7 1389.4 %all-reduce.8.cloned.1.call-start = ((), (), s32[]{:S(2)}) async-start(), calls=%async_computation.13 | async-start | bytes 16777216 | tf_op jit(solution)/shard_map/psum | solution.py:175
  96.1 0.6 copy-start.25
  96.7 81.1 %copy-start.28 = (f32[1024]{0:T(1024)}, f32[1024]{0:T(1024)S(1)}, u32[]{:S(2)}) copy-start(f32[1024]{0:T(1024)S(1)} %fusion.192) | copy-start | bytes 12292
  96.7 7.8 copy-start.38
  100.2 21.8 copy-start.24
  132.9 9.3 copy-start.2
  168.6 9.3 copy-start.3
  1003.5 9.3 copy-start.19
  1003.7 9.0 copy-start.10
  1003.7 9.0 slice-start
  1005.3 7.4 slice-start.1
  1020.1 11.9 copy-start.4
  1020.1 11.9 copy-start.35
  1032.0 14.3 copy-start.23
  1046.2 14.1 copy-start.1
  1046.2 5.2 slice-start.4
  1046.3 5.7 slice-start.5
  1052.0 8.4 copy-start.12
  1060.4 10.3 copy-start.30
  1086.9 10.8 copy-start.44
  1086.9 10.8 copy-start.43
  1108.5 3519.2 %reduce-scatter.13.cloned.1.call-start = ((), (), s32[]{:S(2)}) async-start(), calls=%async_computation.11 | async-start | bytes 5242880 | tf_op jit(solution)/shard_map/reduce_scatter | solution.py:157
  1123.3 3512.8 %reduce-scatter.31.cloned.1.call-start = ((), (), s32[]{:S(2)}) async-start(), calls=%async_computation.22 | async-start | bytes 147456
  1398.1 9.0 copy-start.9
  1398.1 10.2 copy-start.18
  1398.1 19.0 slice-start.2
  1408.3 8.8 slice-start.3
  1432.3 10.9 copy-start.32
  1443.2 8.5 copy-start.20
  1443.2 8.7 copy-start.11
  1473.6 2962.6 %copy-start.34 = (bf16[16,256]{1,0:T(8,128)(2,1)S(1)}, bf16[16,256]{1,0:T(8,128)(2,1)}, u32[]{:S(2)}) copy-start(bf16[16,256]{1,0:T(8,128)(2,1)} %param.33) | copy-start | bytes 24580
  4431.7 8.6 copy-start.29
  4431.7 8.6 copy-start.39
  4431.7 12.6 copy-start.36
  4436.9 15.6 copy-start.21
  4440.2 197.3 %reduce-scatter.21.cloned.1.call-start = ((), (), s32[]{:S(2)}) async-start(), calls=%async_computation.17 | async-start | bytes 147456 | tf_op jit(solution)/shard_map/reduce_scatter | solution.py:240
  4444.3 193.3 %reduce-scatter.23.cloned.1.call-start = ((), (), s32[]{:S(2)}) async-start(), calls=%async_computation.18 | async-start | bytes 4718592 | tf_op jit(solution)/shard_map/reduce_scatter | solution.py:244
  4452.5 185.1 %reduce-scatter.17.cloned.1.call-start = ((), (), s32[]{:S(2)}) async-start(), calls=%async_computation.15 | async-start | bytes 4718592 | tf_op jit(solution)/shard_map/reduce_scatter | solution.py:238
  4460.0 7.7 copy-start.5
  4465.6 2.1 copy-start.13
  4472.5 203.2 %reduce-scatter.15.cloned.1.call-start = ((), (), s32[]{:S(2)}) async-start(), calls=%async_computation.14 | async-start | bytes 4718592 | tf_op jit(solution)/shard_map/reduce_scatter | solution.py:237
  4480.0 7.9 copy-start.6
  4485.9 2.0 copy-start.14
  4492.8 237.9 %reduce-scatter.19.cloned.1.call-start = ((), (), s32[]{:S(2)}) async-start(), calls=%async_computation.16 | async-start | bytes 4718592 | tf_op jit(solution)/shard_map/reduce_scatter | solution.py:239
  4492.8 5.8 copy-start.7
  4496.6 2.0 copy-start.16
  4503.3 318.6 %reduce-scatter.25.cloned.1.call-start = ((), (), s32[]{:S(2)}) async-start(), calls=%async_computation.19 | async-start | bytes 12976128 | tf_op jit(solution)/shard_map/reduce_scatter | solution.py:246
  4515.3 397.7 %reduce-scatter.27.cloned.1.call-start = ((), (), s32[]{:S(2)}) async-start(), calls=%async_computation.20 | async-start | bytes 12976128 | tf_op jit(solution)/shard_map/reduce_scatter | solution.py:247
  4527.5 0.7 copy-start.31
  4527.5 476.5 %reduce-scatter.29.cloned.1.call-start = ((), (), s32[]{:S(2)}) async-start(), calls=%async_computation.21 | async-start | bytes 12976128 | tf_op jit(solution)/shard_map/reduce_scatter | solution.py:248
  4539.6 0.7 copy-start.42
  4539.7 9.9 copy-start.37
  4549.6 12.8 copy-start.15
  4562.4 13.4 copy-start.17
  4575.8 14.4 copy-start.8
  4575.8 14.4 copy-start.22
  4590.2 10.4 copy-start.27
  4590.2 10.4 copy-start.40
  4590.2 36.2 copy-start.26
Sparse Core Ops, SparseCore 0:
  9.6 83.4 all-gather.2
  94.6 79.2 all-gather.4
  1108.6 289.5 all-reduce.7
  1400.3 75.7 reduce-scatter.12
  4440.3 32.6 reduce-scatter.30
  4476.5 33.5 reduce-scatter.20
  4514.0 51.1 reduce-scatter.22
  4569.1 51.4 reduce-scatter.16
  4624.5 51.1 reduce-scatter.14
  4679.5 51.1 reduce-scatter.18
  4734.8 87.1 reduce-scatter.24
  4825.9 87.1 reduce-scatter.26
  4917.1 86.8 reduce-scatter.28
where the time goes:
time: 5100 us; the launch traced here: 5010 us
  matrix products  2080 us (41%)
  local copies, waits for them, and re-layouts  1160 us (23%)
  other arithmetic  985 us (19%)
  waiting for transfers between devices  725 us (14%)
    dot_general x256, matrix products, piece_step(): jnp.einsum('cso,sio->csi', query_rows, key_slot_state, precision=HIGH_PRE...  357 us
    dot_general x256, matrix products, piece_step(): jnp.einsum('thd,jhd->htj', query_rows, key_row_block, precision=HIGH_PREC...  286 us
    psum x1, waiting for transfers between devices, local(): grad_normed_mlp = lax.psum(partial_grad, 'mp')  275 us
    dot_general x256, matrix products, piece_step(): jnp.einsum('eoq,eon->oqn', carried_state, value_row_block, precision=HIGH...  261 us
    dynamic_slice x448, local copies, waits for them, and re-layouts, slot_block(): states, output_rows = lax.scan(piece_step, states, pieces)  258 us
    dot_general x192, matrix products, piece_step(): jnp.einsum('lwe,wez->lwz', attention_probabilities * jnp.exp(running_tota...  236 us
    dynamic_update_slice x320, other arithmetic, slot_block(): states, output_rows = lax.scan(piece_step, states, pieces)  221 us
    dot_general x256, matrix products, piece_step(): jnp.einsum('eoq,eon->oqn', carried_state, key_row_block, precision=HIGH_P...  204 us

commit v1 on v0

--- a/solution.py
+++ b/solution.py
@@ -172,7 +172,11 @@
     grad_gate = rows_product(mlp_low, grad_gate_low)
     grad_up = rows_product(mlp_low, grad_up_low)
     partial_grad = cols_product(grad_gate_low, w_gate) + cols_product(grad_up_low, w_up)
-    grad_normed_mlp = lax.psum(partial_grad, "mp")
+    grad_normed_mlp = partial_grad
+    for hop in (1, 2):
+        grad_normed_mlp = grad_normed_mlp + lax.ppermute(
+            grad_normed_mlp, "mp", [(dev, dev ^ hop) for dev in range(4)]
+        )
     grad_res_mlp, grad_mlp_gain = pull_second(grad_normed_mlp)
     grad_hidden = grad_output + grad_res_mlp
 

time: 5100 us -> 5420 us (1.063)
  waiting for transfers between devices: 725 us -> 1040 us
    ppermute x0 -> x2, waiting for transfers between devices: none -> 597 us  [local(): lax.ppermute(grad_normed_mlp, 'mp', [(dev, dev ^ hop) for dev in range(4)])]
    psum x1 -> x0, waiting for transfers between devices: 275 us -> none  [local(): grad_normed_mlp = lax.psum(partial_grad, 'mp')]
    reduce_scatter x1, waiting for transfers between devices: 91 us -> 0.01 us  [local(): lax.psum_scatter(grad_down, 'dp', scatter_dimension=1, tiled=True)]
    dot_general x256, matrix products: 286 us -> 227 us  [piece_step(): jnp.einsum('thd,jhd->htj', query_rows, key_row_block, precision=HIGH_PREC...]
    dot_general x256, matrix products: 261 us -> 319 us  [piece_step(): jnp.einsum('eoq,eon->oqn', carried_state, value_row_block, precision=HIGH...]
    dot_general x256, matrix products: 204 us -> 147 us  [piece_step(): jnp.einsum('eoq,eon->oqn', carried_state, key_row_block, precision=HIGH_P...]
    dot_general x192, matrix products: 175 us -> 232 us  [piece_step(): jnp.einsum('htj,jhd->thd', mixing, value_row_block, precision=HIGH_PRECIS...]
    reduce_scatter x1, waiting for transfers between devices: 0.01 us -> 55.1 us  [local(): lax.psum_scatter(grad_wout, 'dp', scatter_dimension=0, tiled=True)]
where the time goes in v1:
time: 5420 us; the launch traced here: 5340 us
  matrix products  2080 us (38%)
  local copies, waits for them, and re-layouts  1140 us (21%)
  waiting for transfers between devices  1040 us (19%)
  other arithmetic  1010 us (19%)
    ppermute x2, waiting for transfers between devices, local(): lax.ppermute(grad_normed_mlp, 'mp', [(dev, dev ^ hop) for dev in range(4)])  597 us
    dot_general x256, matrix products, piece_step(): jnp.einsum('cso,sio->csi', query_rows, key_slot_state, precision=HIGH_PRE...  357 us
    dot_general x256, matrix products, piece_step(): jnp.einsum('eoq,eon->oqn', carried_state, value_row_block, precision=HIGH...  319 us
    dynamic_slice x448, local copies, waits for them, and re-layouts, slot_block(): states, output_rows = lax.scan(piece_step, states, pieces)  257 us
    dot_general x192, matrix products, piece_step(): jnp.einsum('lwe,wez->lwz', attention_probabilities * jnp.exp(running_tota...  238 us
    dot_general x192, matrix products, piece_step(): jnp.einsum('htj,jhd->thd', mixing, value_row_block, precision=HIGH_PRECIS...  232 us
    dot_general x256, matrix products, piece_step(): jnp.einsum('thd,jhd->htj', query_rows, key_row_block, precision=HIGH_PREC...  227 us
    dynamic_update_slice x320, other arithmetic, slot_block(): states, output_rows = lax.scan(piece_step, states, pieces)  223 us

profile of v1, /device:TPU:0, one launch (start us, length us, event | category | flops | bytes accessed | tf_op | source)
XLA Modules:
  0.0 5336.6 jit_solution(3421227339502219328)
XLA Ops:
  11.3 81.8 %all-gather.3.cloned.1.call-done = bf16[1024,2048]{1,0:T(8,128)(2,1)} async-done(((bf16[256,2048]{1,0:T(8,128)(2,1)}), bf16[1024,2048]{1,0:T(8,128)(2,1)}) %all-gather.3.cloned.1.call-update) | async-done | bytes 4194320 | tf_op jit(solution)/shard_map/all_gather | solution.py:116
  104.5 15.1 convert_convert_fusion
  119.6 10.8 reshape.460
  130.5 9.3 copy.327
  139.8 15.4 fusion.174
  155.2 11.0 reshape.459
  166.3 9.3 copy.326
  175.5 15.4 fusion.173
  190.9 10.8 reshape.458
  216.6 765.9 %while.238 = (s32[]{:T(128)}, f32[4,64,512]{2,1,0:T(8,128)S(1)}, f32[4,64,512]{2,1,0:T(8,128)}, f32[8,128,4,512]{3,2,1,0:T(4,128)}, f32[8,4,64,512]{3,2,1,0:T(8,...) while((s32[]{:T(128)}, f32[4,64,512]{2,1,0:T(8,128)S(1)}, ...), condition=%wide.region_7.8_spmd.clone.clone, body=%wide.region_1.7_spmd.clone.clone.sunk | while | flops 115744832 | bytes 22997152 | solution.py:92
  224.0 83.1 %while.241 = (s32[]{:T(128)}, f32[4,64,512]{2,1,0:T(8,128)S(1)}, f32[4,64,512]{2,1,0:T(8,128)S(1)}, f32[8,16,4,512]{3,2,1,0:T(4,128)}, f32[8,16,4,64]{3,2,1,0:T(...) while((s32[]{:T(128)}, f32[4,64,512]{2,1,0:T(8,128)S(1)}, ...), condition=%wide.region_6.6_spmd.clone, body=%wide.region_2.5_spmd.clone.sunk | while | flops 115744832 | bytes 5891725 | solution.py:77
  319.6 83.1 %while.241 = (s32[]{:T(128)}, f32[4,64,512]{2,1,0:T(8,128)S(1)}, f32[4,64,512]{2,1,0:T(8,128)S(1)}, f32[8,16,4,512]{3,2,1,0:T(4,128)}, f32[8,16,4,64]{3,2,1,0:T(...) while((s32[]{:T(128)}, f32[4,64,512]{2,1,0:T(8,128)S(1)}, ...), condition=%wide.region_6.6_spmd.clone, body=%wide.region_2.5_spmd.clone.sunk | while | flops 115744832 | bytes 5891725 | solution.py:77
  415.3 83.1 %while.241 = (s32[]{:T(128)}, f32[4,64,512]{2,1,0:T(8,128)S(1)}, f32[4,64,512]{2,1,0:T(8,128)S(1)}, f32[8,16,4,512]{3,2,1,0:T(4,128)}, f32[8,16,4,64]{3,2,1,0:T(...) while((s32[]{:T(128)}, f32[4,64,512]{2,1,0:T(8,128)S(1)}, ...), condition=%wide.region_6.6_spmd.clone, body=%wide.region_2.5_spmd.clone.sunk | while | flops 115744832 | bytes 5891725 | solution.py:77
  511.0 83.1 %while.241 = (s32[]{:T(128)}, f32[4,64,512]{2,1,0:T(8,128)S(1)}, f32[4,64,512]{2,1,0:T(8,128)S(1)}, f32[8,16,4,512]{3,2,1,0:T(4,128)}, f32[8,16,4,64]{3,2,1,0:T(...) while((s32[]{:T(128)}, f32[4,64,512]{2,1,0:T(8,128)S(1)}, ...), condition=%wide.region_6.6_spmd.clone, body=%wide.region_2.5_spmd.clone.sunk | while | flops 115744832 | bytes 5891725 | solution.py:77
  606.7 83.1 %while.241 = (s32[]{:T(128)}, f32[4,64,512]{2,1,0:T(8,128)S(1)}, f32[4,64,512]{2,1,0:T(8,128)S(1)}, f32[8,16,4,512]{3,2,1,0:T(4,128)}, f32[8,16,4,64]{3,2,1,0:T(...) while((s32[]{:T(128)}, f32[4,64,512]{2,1,0:T(8,128)S(1)}, ...), condition=%wide.region_6.6_spmd.clone, body=%wide.region_2.5_spmd.clone.sunk | while | flops 115744832 | bytes 5891725 | solution.py:77
  702.4 83.1 %while.241 = (s32[]{:T(128)}, f32[4,64,512]{2,1,0:T(8,128)S(1)}, f32[4,64,512]{2,1,0:T(8,128)S(1)}, f32[8,16,4,512]{3,2,1,0:T(4,128)}, f32[8,16,4,64]{3,2,1,0:T(...) while((s32[]{:T(128)}, f32[4,64,512]{2,1,0:T(8,128)S(1)}, ...), condition=%wide.region_6.6_spmd.clone, body=%wide.region_2.5_spmd.clone.sunk | while | flops 115744832 | bytes 5891725 | solution.py:77
  798.1 83.1 %while.241 = (s32[]{:T(128)}, f32[4,64,512]{2,1,0:T(8,128)S(1)}, f32[4,64,512]{2,1,0:T(8,128)S(1)}, f32[8,16,4,512]{3,2,1,0:T(4,128)}, f32[8,16,4,64]{3,2,1,0:T(...) while((s32[]{:T(128)}, f32[4,64,512]{2,1,0:T(8,128)S(1)}, ...), condition=%wide.region_6.6_spmd.clone, body=%wide.region_2.5_spmd.clone.sunk | while | flops 115744832 | bytes 5891725 | solution.py:77
  894.0 83.1 %while.241 = (s32[]{:T(128)}, f32[4,64,512]{2,1,0:T(8,128)S(1)}, f32[4,64,512]{2,1,0:T(8,128)S(1)}, f32[8,16,4,512]{3,2,1,0:T(4,128)}, f32[8,16,4,64]{3,2,1,0:T(...) while((s32[]{:T(128)}, f32[4,64,512]{2,1,0:T(8,128)S(1)}, ...), condition=%wide.region_6.6_spmd.clone, body=%wide.region_2.5_spmd.clone.sunk | while | flops 115744832 | bytes 5891725 | solution.py:77
  1004.8 11.9 mul.733
  1016.7 14.2 multiply_reduce_fusion.6
  1031.8 15.0 fusion.209
  1055.3 16.0 multiply_convert_fusion.7
  1071.2 10.8 fusion.210
  1082.1 9.7 convolution_add_fusion.9
  1095.0 182.1 %collective-permute-done = f32[1024,2048]{1,0:T(8,128)} collective-permute-done((f32[1024,2048]{1,0:T(8,128)S(1)}, f32[1024,2048]{1,0:T(8,128)}, u32[]{:S(2)}, u32[]{:S(2)}) %collective-permute-start) | collective-permute-done | bytes 8388640 | tf_op jit(solution)/shard_map/ppermute | solution.py:177
  1277.2 11.8 add.261
  1293.2 10.8 convolution_convert_fusion
  1304.0 414.6 %collective-permute-done.1 = f32[1024,2048]{1,0:T(8,128)} collective-permute-done((f32[1024,2048]{1,0:T(8,128)}, f32[1024,2048]{1,0:T(8,128)}, u32[]{:S(2)}, u32[]{:S(2)}) %collective-permute-start.1) | collective-permute-done | bytes 8388640 | tf_op jit(solution)/shard_map/ppermute | solution.py:177
  1718.6 11.0 multiply_reduce_fusion
  1729.5 14.6 fusion.204
  1744.2 15.1 multiply_reduce_fusion.1
  1759.3 10.8 reshape.446
  1778.8 10.4 add_add_fusion
  1800.6 2956.7 %while.236 = (s32[]{:T(128)}, f32[4,64,512]{2,1,0:T(8,128)S(1)}, f32[4,64,512]{2,1,0:T(8,128)S(1)}, f32[8,128,4,512]{3,2,1,0:T(4,128)}, f32[8,128,4,512]{3,2,1,0...) while((s32[]{:T(128)}, f32[4,64,512]{2,1,0:T(8,128)S(1)}, ...), condition=%wide.region_29.30_spmd, body=%wide.region_13.0_spmd.sunk | while | flops 314950080 | bytes 50764040 | solution.py:92
  1817.3 117.3 %while.239 = (s32[]{:T(128)}, f32[4,64,512]{2,1,0:T(8,128)S(1)}, f32[4,64,512]{2,1,0:T(8,128)S(1)}, f32[8,4,64]{2,1,0:T(4,128)S(1)}, f32[8,4,64,512]{3,2,1,0:T(8...) while((s32[]{:T(128)}, f32[4,64,512]{2,1,0:T(8,128)S(1)}, ...), condition=%wide.region_18.18_spmd.clone.clone, body=%wide.region_14.17_spmd.clone.clone.sunk | while | flops 84529344 | bytes 8696389 | solution.py:77
  1936.9 227.2 %while.240 = (s32[]{:T(128)}, f32[4,64,512]{2,1,0:T(8,128)S(1)}, f32[4,64,512]{2,1,0:T(8,128)S(1)}, f32[8,16,4,512]{3,2,1,0:T(4,128)}, f32[8,16,4,512]{3,2,1,0:T...) while((s32[]{:T(128)}, f32[4,64,512]{2,1,0:T(8,128)S(1)}, ...), condition=%wide.region_28.28_spmd.clone.clone, body=%wide.region_19.27_spmd.clone.clone.sunk | while | flops 230158336 | bytes 13886109 | solution.py:77
  2186.8 117.3 %while.239 = (s32[]{:T(128)}, f32[4,64,512]{2,1,0:T(8,128)S(1)}, f32[4,64,512]{2,1,0:T(8,128)S(1)}, f32[8,4,64]{2,1,0:T(4,128)S(1)}, f32[8,4,64,512]{3,2,1,0:T(8...) while((s32[]{:T(128)}, f32[4,64,512]{2,1,0:T(8,128)S(1)}, ...), condition=%wide.region_18.18_spmd.clone.clone, body=%wide.region_14.17_spmd.clone.clone.sunk | while | flops 84529344 | bytes 8696389 | solution.py:77
  2306.5 227.2 %while.240 = (s32[]{:T(128)}, f32[4,64,512]{2,1,0:T(8,128)S(1)}, f32[4,64,512]{2,1,0:T(8,128)S(1)}, f32[8,16,4,512]{3,2,1,0:T(4,128)}, f32[8,16,4,512]{3,2,1,0:T...) while((s32[]{:T(128)}, f32[4,64,512]{2,1,0:T(8,128)S(1)}, ...), condition=%wide.region_28.28_spmd.clone.clone, body=%wide.region_19.27_spmd.clone.clone.sunk | while | flops 230158336 | bytes 13886109 | solution.py:77
  2556.4 117.3 %while.239 = (s32[]{:T(128)}, f32[4,64,512]{2,1,0:T(8,128)S(1)}, f32[4,64,512]{2,1,0:T(8,128)S(1)}, f32[8,4,64]{2,1,0:T(4,128)S(1)}, f32[8,4,64,512]{3,2,1,0:T(8...) while((s32[]{:T(128)}, f32[4,64,512]{2,1,0:T(8,128)S(1)}, ...), condition=%wide.region_18.18_spmd.clone.clone, body=%wide.region_14.17_spmd.clone.clone.sunk | while | flops 84529344 | bytes 8696389 | solution.py:77
  2676.0 227.2 %while.240 = (s32[]{:T(128)}, f32[4,64,512]{2,1,0:T(8,128)S(1)}, f32[4,64,512]{2,1,0:T(8,128)S(1)}, f32[8,16,4,512]{3,2,1,0:T(4,128)}, f32[8,16,4,512]{3,2,1,0:T...) while((s32[]{:T(128)}, f32[4,64,512]{2,1,0:T(8,128)S(1)}, ...), condition=%wide.region_28.28_spmd.clone.clone, body=%wide.region_19.27_spmd.clone.clone.sunk | while | flops 230158336 | bytes 13886109 | solution.py:77
  2925.9 117.3 %while.239 = (s32[]{:T(128)}, f32[4,64,512]{2,1,0:T(8,128)S(1)}, f32[4,64,512]{2,1,0:T(8,128)S(1)}, f32[8,4,64]{2,1,0:T(4,128)S(1)}, f32[8,4,64,512]{3,2,1,0:T(8...) while((s32[]{:T(128)}, f32[4,64,512]{2,1,0:T(8,128)S(1)}, ...), condition=%wide.region_18.18_spmd.clone.clone, body=%wide.region_14.17_spmd.clone.clone.sunk | while | flops 84529344 | bytes 8696389 | solution.py:77
  3045.6 227.2 %while.240 = (s32[]{:T(128)}, f32[4,64,512]{2,1,0:T(8,128)S(1)}, f32[4,64,512]{2,1,0:T(8,128)S(1)}, f32[8,16,4,512]{3,2,1,0:T(4,128)}, f32[8,16,4,512]{3,2,1,0:T...) while((s32[]{:T(128)}, f32[4,64,512]{2,1,0:T(8,128)S(1)}, ...), condition=%wide.region_28.28_spmd.clone.clone, body=%wide.region_19.27_spmd.clone.clone.sunk | while | flops 230158336 | bytes 13886109 | solution.py:77
  3295.5 117.3 %while.239 = (s32[]{:T(128)}, f32[4,64,512]{2,1,0:T(8,128)S(1)}, f32[4,64,512]{2,1,0:T(8,128)S(1)}, f32[8,4,64]{2,1,0:T(4,128)S(1)}, f32[8,4,64,512]{3,2,1,0:T(8...) while((s32[]{:T(128)}, f32[4,64,512]{2,1,0:T(8,128)S(1)}, ...), condition=%wide.region_18.18_spmd.clone.clone, body=%wide.region_14.17_spmd.clone.clone.sunk | while | flops 84529344 | bytes 8696389 | solution.py:77
  3415.1 227.2 %while.240 = (s32[]{:T(128)}, f32[4,64,512]{2,1,0:T(8,128)S(1)}, f32[4,64,512]{2,1,0:T(8,128)S(1)}, f32[8,16,4,512]{3,2,1,0:T(4,128)}, f32[8,16,4,512]{3,2,1,0:T...) while((s32[]{:T(128)}, f32[4,64,512]{2,1,0:T(8,128)S(1)}, ...), condition=%wide.region_28.28_spmd.clone.clone, body=%wide.region_19.27_spmd.clone.clone.sunk | while | flops 230158336 | bytes 13886109 | solution.py:77
  3665.0 117.3 %while.239 = (s32[]{:T(128)}, f32[4,64,512]{2,1,0:T(8,128)S(1)}, f32[4,64,512]{2,1,0:T(8,128)S(1)}, f32[8,4,64]{2,1,0:T(4,128)S(1)}, f32[8,4,64,512]{3,2,1,0:T(8...) while((s32[]{:T(128)}, f32[4,64,512]{2,1,0:T(8,128)S(1)}, ...), condition=%wide.region_18.18_spmd.clone.clone, body=%wide.region_14.17_spmd.clone.clone.sunk | while | flops 84529344 | bytes 8696389 | solution.py:77
  3784.7 227.2 %while.240 = (s32[]{:T(128)}, f32[4,64,512]{2,1,0:T(8,128)S(1)}, f32[4,64,512]{2,1,0:T(8,128)S(1)}, f32[8,16,4,512]{3,2,1,0:T(4,128)}, f32[8,16,4,512]{3,2,1,0:T...) while((s32[]{:T(128)}, f32[4,64,512]{2,1,0:T(8,128)S(1)}, ...), condition=%wide.region_28.28_spmd.clone.clone, body=%wide.region_19.27_spmd.clone.clone.sunk | while | flops 230158336 | bytes 13886109 | solution.py:77
  4034.6 117.3 %while.239 = (s32[]{:T(128)}, f32[4,64,512]{2,1,0:T(8,128)S(1)}, f32[4,64,512]{2,1,0:T(8,128)S(1)}, f32[8,4,64]{2,1,0:T(4,128)S(1)}, f32[8,4,64,512]{3,2,1,0:T(8...) while((s32[]{:T(128)}, f32[4,64,512]{2,1,0:T(8,128)S(1)}, ...), condition=%wide.region_18.18_spmd.clone.clone, body=%wide.region_14.17_spmd.clone.clone.sunk | while | flops 84529344 | bytes 8696389 | solution.py:77
  4154.2 227.2 %while.240 = (s32[]{:T(128)}, f32[4,64,512]{2,1,0:T(8,128)S(1)}, f32[4,64,512]{2,1,0:T(8,128)S(1)}, f32[8,16,4,512]{3,2,1,0:T(4,128)}, f32[8,16,4,512]{3,2,1,0:T...) while((s32[]{:T(128)}, f32[4,64,512]{2,1,0:T(8,128)S(1)}, ...), condition=%wide.region_28.28_spmd.clone.clone, body=%wide.region_19.27_spmd.clone.clone.sunk | while | flops 230158336 | bytes 13886109 | solution.py:77
  4404.1 117.3 %while.239 = (s32[]{:T(128)}, f32[4,64,512]{2,1,0:T(8,128)S(1)}, f32[4,64,512]{2,1,0:T(8,128)S(1)}, f32[8,4,64]{2,1,0:T(4,128)S(1)}, f32[8,4,64,512]{3,2,1,0:T(8...) while((s32[]{:T(128)}, f32[4,64,512]{2,1,0:T(8,128)S(1)}, ...), condition=%wide.region_18.18_spmd.clone.clone, body=%wide.region_14.17_spmd.clone.clone.sunk | while | flops 84529344 | bytes 8696389 | solution.py:77
  4523.8 227.2 %while.240 = (s32[]{:T(128)}, f32[4,64,512]{2,1,0:T(8,128)S(1)}, f32[4,64,512]{2,1,0:T(8,128)S(1)}, f32[8,16,4,512]{3,2,1,0:T(4,128)}, f32[8,16,4,512]{3,2,1,0:T...) while((s32[]{:T(128)}, f32[4,64,512]{2,1,0:T(8,128)S(1)}, ...), condition=%wide.region_28.28_spmd.clone.clone, body=%wide.region_19.27_spmd.clone.clone.sunk | while | flops 230158336 | bytes 13886109 | solution.py:77
  4770.0 11.7 fusion.176
  4781.8 11.9 fusion.215
  4793.7 12.1 fusion.214
  4878.8 14.7 fusion.213
  4893.6 15.2 fusion.212
  4908.8 13.6 fusion.211
  4922.4 9.9 multiply_reduce_fusion.2
  4932.5 24.5 all-reduce.5
  4965.5 52.6 reduce-scatter.27.cloned.1.call-done
  5018.1 91.2 %reduce-scatter.25.cloned.1.call-done = f32[256,1408]{1,0:T(8,128)} async-done(((f32[2048,1408]{1,0:T(8,128)}), f32[256,1408]{1,0:T(8,128)}) %reduce-scatter.25.cloned.1.call-update) | async-done | bytes 1441808 | tf_op jit(solution)/shard_map/reduce_scatter | solution.py:250
  5109.3 55.1 %reduce-scatter.23.cloned.1.call-done = f32[256,512]{1,0:T(8,128)} async-done(((f32[2048,512]{1,0:T(8,128)}), f32[256,512]{1,0:T(8,128)}) %reduce-scatter.23.cloned.1.call-update) | async-done | bytes 524304 | tf_op jit(solution)/shard_map/reduce_scatter | solution.py:248
  5164.4 55.0 %reduce-scatter.19.cloned.1.call-done = f32[256,512]{1,0:T(8,128)} async-done(((f32[2048,512]{1,0:T(8,128)}), f32[256,512]{1,0:T(8,128)}) %reduce-scatter.19.cloned.1.call-update) | async-done | bytes 524304 | tf_op jit(solution)/shard_map/reduce_scatter | solution.py:243
  5219.4 55.1 %reduce-scatter.17.cloned.1.call-done = f32[256,512]{1,0:T(8,128)} async-done(((f32[2048,512]{1,0:T(8,128)}), f32[256,512]{1,0:T(8,128)}) %reduce-scatter.17.cloned.1.call-update) | async-done | bytes 524304 | tf_op jit(solution)/shard_map/reduce_scatter | solution.py:242
  5274.6 55.0 %reduce-scatter.15.cloned.1.call-done = f32[256,512]{1,0:T(8,128)} async-done(((f32[2048,512]{1,0:T(8,128)}), f32[256,512]{1,0:T(8,128)}) %reduce-scatter.15.cloned.1.call-update) | async-done | bytes 524304 | tf_op jit(solution)/shard_map/reduce_scatter | solution.py:241
  (5817 shorter events, 3883.6 us)
Async XLA Ops:
  7.2 89.5 %copy-start = (bf16[2048,16]{0,1:T(8,128)(2,1)S(1)}, bf16[2048,16]{0,1:T(8,128)(2,1)}, u32[]{:S(2)}) copy-start(bf16[2048,16]{0,1:T(8,128)(2,1)} %param.32) | copy-start | bytes 196612
  7.2 85.9 %all-gather.3.cloned.1.call-start = ((), (), s32[]{:S(2)}) async-start(), calls=%async_computation.10 | async-start | bytes 5242880 | tf_op jit(solution)/shard_map/all_gather | solution.py:116
  7.9 92.3 %copy-start.33 = (bf16[16,256]{1,0:T(8,128)(2,1)S(1)}, bf16[16,256]{1,0:T(8,128)(2,1)}, u32[]{:S(2)}) copy-start(bf16[16,256]{1,0:T(8,128)(2,1)} %param.33) | copy-start | bytes 24580
  7.9 92.3 %copy-start.41 = (f32[256]{0:T(256)S(1)}, f32[256]{0:T(256)}, u32[]{:S(2)}) copy-start(f32[256]{0:T(256)} %param.34) | copy-start | bytes 3076
  8.0 1047.3 %all-gather.5.cloned.1.call-start = ((), (), s32[]{:S(2)}) async-start(), calls=%async_computation.12 | async-start | bytes 5242880 | tf_op jit(solution)/shard_map/all_gather | solution.py:117
  8.7 4848.6 %reduce-scatter.13.cloned.1.call-start = ((), (), s32[]{:S(2)}) async-start(), calls=%async_computation.11 | async-start | bytes 5242880 | tf_op jit(solution)/shard_map/reduce_scatter | solution.py:157
  96.7 78.8 %copy-start.28 = (f32[1024]{0:T(1024)}, f32[1024]{0:T(1024)S(1)}, u32[]{:S(2)}) copy-start(f32[1024]{0:T(1024)S(1)} %fusion.192) | copy-start | bytes 12292
  96.7 7.8 copy-start.38
  100.2 19.4 copy-start.24
  130.5 9.3 copy-start.3
  166.3 9.3 copy-start.4
  216.8 3.1 copy-start.2
  987.8 9.6 copy-start.19
  988.1 9.4 copy-start.11
  988.1 9.3 slice-start
  989.9 7.5 slice-start.1
  1004.8 11.9 copy-start.5
  1004.8 11.9 copy-start.35
  1016.7 14.3 copy-start.23
  1031.0 15.8 copy-start.1
  1031.0 15.8 slice-start.8
  1031.8 15.0 copy-start.14
  1031.8 15.0 slice-start.9
  1046.8 8.5 copy-start.30
  1071.2 10.8 copy-start.44
  1071.2 221.9 %copy-start.43 = (bf16[1024,1408]{1,0:T(8,128)(2,1)}, bf16[1024,1408]{1,0:T(8,128)(2,1)S(1)}, u32[]{:S(2)}) copy-start(bf16[1024,1408]{1,0:T(8,128)(2,1)S(1)} %get-tuple-element.3183) | copy-start | bytes 8650756
  1091.8 3.2 copy-start.10
  1095.0 182.1 %collective-permute-start = (f32[1024,2048]{1,0:T(8,128)S(1)}, f32[1024,2048]{1,0:T(8,128)}, u32[]{:S(2)}, u32[]{:S(2)}) collective-permute-start(f32[1024,2048]{1,0:T(8,128)S(1)} %convolution_add_fusion.9), channel_id=1, source_target_pairs={{0,1},{1,0},{2,3},{3,2},{4,5},{5,4},{6,7},{7,6},{8,9},{9,8},{10,11... | collective-permute-start | bytes 25165832 | tf_op jit(solution)/shard_map/ppermute | solution.py:177
  1289.0 429.6 %collective-permute-start.1 = (f32[1024,2048]{1,0:T(8,128)}, f32[1024,2048]{1,0:T(8,128)}, u32[]{:S(2)}, u32[]{:S(2)}) collective-permute-start(f32[1024,2048]{1,0:T(8,128)} %add.261), channel_id=1, source_target_pairs={{0,2},{1,3},{2,0},{3,1},{4,6},{5,7},{6,4},{7,5},{8,10},{9,11},{10,... | collective-permute-start | bytes 25165832 | tf_op jit(solution)/shard_map/ppermute | solution.py:177
  1304.0 3660.2 %reduce-scatter.31.cloned.1.call-start = ((), (), s32[]{:S(2)}) async-start(), calls=%async_computation.21 | async-start | bytes 147456
  1304.0 425.5 %copy-start.13 = (bf16[1024,2048]{1,0:T(8,128)(2,1)S(1)}, bf16[1024,2048]{1,0:T(8,128)(2,1)}, u32[]{:S(2)}) copy-start(bf16[1024,2048]{1,0:T(8,128)(2,1)} %all-gather.5.cloned.1.call-done) | copy-start | bytes 12582916
  1718.6 25.6 slice-start.2
  1729.5 14.6 slice-start.3
  1759.3 10.8 copy-start.32
  1770.1 8.4 copy-start.20
  1770.1 8.7 copy-start.12
  1800.6 2961.4 %copy-start.34 = (bf16[16,256]{1,0:T(8,128)(2,1)S(1)}, bf16[16,256]{1,0:T(8,128)(2,1)}, u32[]{:S(2)}) copy-start(bf16[16,256]{1,0:T(8,128)(2,1)} %param.33) | copy-start | bytes 24580
  4757.4 8.6 copy-start.29
  4757.4 8.6 copy-start.39
  4757.4 12.6 copy-start.31
  4762.6 19.1 copy-start.21
  4765.9 199.6 %reduce-scatter.21.cloned.1.call-start = ((), (), s32[]{:S(2)}) async-start(), calls=%async_computation.16 | async-start | bytes 147456 | tf_op jit(solution)/shard_map/reduce_scatter | solution.py:244
  4770.0 195.5 %reduce-scatter.29.cloned.1.call-start = ((), (), s32[]{:S(2)}) async-start(), calls=%async_computation.20 | async-start | bytes 12976128 | tf_op jit(solution)/shard_map/reduce_scatter | solution.py:252
  4781.7 236.3 %reduce-scatter.27.cloned.1.call-start = ((), (), s32[]{:S(2)}) async-start(), calls=%async_computation.19 | async-start | bytes 12976128 | tf_op jit(solution)/shard_map/reduce_scatter | solution.py:251
  4793.7 315.6 %reduce-scatter.25.cloned.1.call-start = ((), (), s32[]{:S(2)}) async-start(), calls=%async_computation.18 | async-start | bytes 12976128 | tf_op jit(solution)/shard_map/reduce_scatter | solution.py:250
  4805.8 358.6 %reduce-scatter.23.cloned.1.call-start = ((), (), s32[]{:S(2)}) async-start(), calls=%async_computation.17 | async-start | bytes 4718592 | tf_op jit(solution)/shard_map/reduce_scatter | solution.py:248
  4814.7 404.7 %reduce-scatter.19.cloned.1.call-start = ((), (), s32[]{:S(2)}) async-start(), calls=%async_computation.15 | async-start | bytes 4718592 | tf_op jit(solution)/shard_map/reduce_scatter | solution.py:243
  4814.8 5.8 copy-start.6
  4825.3 449.2 %reduce-scatter.17.cloned.1.call-start = ((), (), s32[]{:S(2)}) async-start(), calls=%async_computation.14 | async-start | bytes 4718592 | tf_op jit(solution)/shard_map/reduce_scatter | solution.py:242
  4833.1 7.4 copy-start.7
  4840.5 4.9 copy-start.42
  4845.3 484.3 %reduce-scatter.15.cloned.1.call-start = ((), (), s32[]{:S(2)}) async-start(), calls=%async_computation.13 | async-start | bytes 4718592 | tf_op jit(solution)/shard_map/reduce_scatter | solution.py:241
  4857.3 11.2 slice-start.4
  4860.7 7.7 slice-start.5
  4868.4 5.6 copy-start.8
  4878.8 14.7 copy-start.37
  4893.6 15.2 copy-start.17
  4893.6 28.8 slice-start.6
  4908.8 13.6 copy-start.9
  4908.8 13.6 slice-start.7
  4908.8 13.6 copy-start.22
  4922.4 10.0 copy-start.26
  4922.4 10.1 copy-start.27
  4922.4 10.1 copy-start.40
  (12 other events, 29.0 us)
Sparse Core Ops, SparseCore 0:
  9.6 83.4 all-gather.2
  94.6 79.2 all-gather.4
  1304.1 254.9 reduce-scatter.12
  4766.0 32.9 reduce-scatter.30
  4802.4 33.5 reduce-scatter.20
  4839.9 86.8 reduce-scatter.28
  4930.9 87.1 reduce-scatter.26
  5022.1 87.1 reduce-scatter.24
  5113.2 51.1 reduce-scatter.22
  5168.2 51.1 reduce-scatter.18
  5223.4 51.1 reduce-scatter.16
  5278.3 51.1 reduce-scatter.14
